TPU v7x, 32 devices: a whole 2x2x4 slice. The times are simulated.
32 devices in a mesh: dp: 4 (over x, core), ctx: 4 (over z), tensor: 2 (over y).
Axes of the slice: x: 2, y: 2, z: 4, core: 2. Of those that a mesh axis runs over, the one named last changes fastest.
Arguments:
- block_input: bfloat16 [12288, 2048], P(('dp', 'ctx'), 'tensor'), may hold values from -6 to 6
- cotangent: bfloat16 [12288, 2048], P(('dp', 'ctx'), 'tensor'), may hold values from -6 to 6
- deal_order: int32 [4, 4], P('dp'), may hold values from 0 to 3, as said below
- seq_lengths: int32 [12], P('dp'), may hold values from 96 to 2880, as said below
- seq_adapter: int32 [12], P('dp'), may hold values from 0 to 7
- mixer_gain: bfloat16 [2048], replicated, may hold values from 0.099609375 to 1.8984375
- ffn_gain: bfloat16 [2048], replicated, may hold values from 0.099609375 to 1.8984375
- conv_taps: bfloat16 [3, 2048], P(None, 'tensor'), may hold values from -3.5 to 3.5
- in_weight: bfloat16 [3, 2048, 2048], P(None, 'dp', 'tensor'), may hold values from -0.125 to 0.125
- out_weight: bfloat16 [2048, 2048], P('tensor', 'dp'), may hold values from -0.125 to 0.125
- gateup_weight: bfloat16 [2, 2048, 5632], P(None, 'dp', 'tensor'), may hold values from -0.125 to 0.125
- down_weight: bfloat16 [5632, 2048], P('tensor', 'dp'), may hold values from -0.078125 to 0.078125
- input_adapter_shrink: bfloat16 [2048, 128], replicated, may hold values from -0.125 to 0.125
- in_expand: bfloat16 [3, 128, 2048], P(None, None, 'tensor'), may hold values from -1.5 to 1.5
- out_shrink: bfloat16 [2048, 128], P('tensor'), may hold values from -0.125 to 0.125
- output_adapter_expand: bfloat16 [128, 2048], replicated, may hold values from -1.5 to 1.5
- ffn_shrink: bfloat16 [2048, 256], replicated, may hold values from -0.125 to 0.125
- ffn_expand: bfloat16 [2, 128, 5632], P(None, None, 'tensor'), may hold values from -1.5 to 1.5
- down_shrink: bfloat16 [5632, 128], P('tensor'), may hold values from -0.078125 to 0.078125
- down_adapter_expand: bfloat16 [128, 2048], replicated, may hold values from -1.5 to 1.5
Outputs:
- block_output: bfloat16 [12288, 2048], P(('dp', 'ctx'), 'tensor')
- input_grad: float32 [12288, 2048], P(('dp', 'ctx'), 'tensor')
- in_shrink_grad: float32 [2048, 128], replicated
- input_expand_gradient: float32 [3, 128, 2048], P(None, None, 'tensor')
- out_shrink_grad: float32 [2048, 128], P('tensor')
- output_expand_gradient: float32 [128, 2048], replicated
- ffn_shrink_grad: float32 [2048, 256], replicated
- feedforward_expand_gradient: float32 [2, 128, 5632], P(None, None, 'tensor')
- down_shrink_grad: float32 [5632, 128], P('tensor')
- down_adapter_expand_gradient: float32 [128, 2048], replicated
Inputs may be any that keep to these rules, and one draw needn't show every extreme that they name: `deal_order`: each row is a permutation of the 4 shard numbers. `seq_lengths`: each data group's 3 entries sum to 3072; all but one of them lie between 96 and 192.
All inputs are finite; a program needn't handle non-finite values.
Results may differ from a plain program's by a relative error of at most 0.013.
Values may be sent and summed in bfloat16 or wider, within the bound.
No kernel may reach another device: no remote copies, remote signals or barrier semaphores. Data moves between devices by JAX's collectives and lax.ppermute only.
A program may use at most 256 MiB of HBM per device.

v0:
```python
import jax
import jax.numpy as jnp
from jax import lax
from jax.sharding import PartitionSpec as P

RANK = 16
norm_eps = 1e-05
adapter_scale = 0.5


def shifted(block, axis, distance):
    devices = range(lax.axis_size(axis))
    route = [(i - distance, i) for i in devices if i - distance in devices]
    return lax.ppermute(block, axis, route)


def rms_scale(values):
    return lax.rsqrt(jnp.mean(values * values, axis=-1, keepdims=True) + norm_eps)


def norm_back(values, scale, gain, grad_out):
    unit = values * scale
    grad_unit = grad_out * gain
    return scale * (grad_unit - unit * jnp.mean(grad_unit * unit, axis=-1, keepdims=True))


def product_simple(left, right):
    return jnp.dot(left, right, preferred_element_type=jnp.float32)


def product_backward(left, right):
    return lax.dot_general(
        left, right, (((1,), (1,)), ((), ())), preferred_element_type=jnp.float32
    )


def product_leading(left, right):
    return lax.dot_general(
        left, right, (((0,), (0,)), ((), ())), preferred_element_type=jnp.float32
    )


def segment_of(positions, seq_ends):
    return jnp.sum((positions[:, None] >= seq_ends[None, :]).astype(jnp.int32), axis=1)


def fetch_mixer(in_weight, out_weight):
    return (
        lax.all_gather(in_weight, "dp", axis=1, tiled=True),
        lax.all_gather(out_weight, "dp", axis=1, tiled=True),
    )


def fetch_ffn(gateup_weight, down_weight):
    return (
        lax.all_gather(gateup_weight, "dp", axis=1, tiled=True),
        lax.all_gather(down_weight, "dp", axis=1, tiled=True),
    )


def body(
    block_input,
    cotangent,
    deal_order,
    seq_lengths,
    seq_adapter,
    mixer_gain,
    ffn_gain,
    conv_taps,
    in_weight,
    out_weight,
    gateup_weight,
    down_weight,
    input_adapter_shrink,
    in_expand,
    out_shrink,
    output_adapter_expand,
    ffn_shrink,
    ffn_expand,
    down_shrink,
    down_adapter_expand,
):
    tok_count = block_input.shape[0]
    half_width = block_input.shape[1]
    rank_cols = input_adapter_shrink.shape[1]
    part_index = lax.axis_index("tensor")
    group_total = lax.axis_size("dp")
    block_rows = tok_count // group_total
    deal_row = deal_order[0]
    slot_all = jnp.arange(group_total, dtype=jnp.int32)
    inverse_row = jnp.sum(
        jnp.where(deal_row[:, None] == slot_all[None, :], slot_all[:, None], 0), axis=0
    )
    dealt_in, dealt_cot = (
        lax.all_to_all(
            block_input.reshape(group_total, block_rows, half_width),
            "dp",
            split_axis=0,
            concat_axis=0,
            tiled=True,
        ),
        lax.all_to_all(
            cotangent.reshape(group_total, block_rows, half_width),
            "dp",
            split_axis=0,
            concat_axis=0,
            tiled=True,
        ),
    )
    packed_in = jnp.take(dealt_in, deal_row, axis=0).reshape(tok_count, half_width)
    packed_cot = jnp.take(dealt_cot, deal_row, axis=0).reshape(tok_count, half_width)
    seq_ends = jnp.cumsum(seq_lengths)[:-1]
    positions = lax.axis_index("ctx") * tok_count + jnp.arange(tok_count, dtype=jnp.int32)
    segment = segment_of(positions, seq_ends)
    slot_ids = jnp.arange(seq_lengths.shape[0], dtype=jnp.int32)
    token_adapter_index = jnp.sum(
        jnp.where(segment[:, None] == slot_ids[None, :], seq_adapter[None, :], 0), axis=1
    )
    column_group_index = jnp.arange(rank_cols, dtype=jnp.int32) // RANK
    adapter_mask = (column_group_index[None, :] == token_adapter_index[:, None]).astype(jnp.float32)
    adapter_half_float = adapter_mask.astype(jnp.bfloat16)
    adapter_mask_pair = jnp.concatenate([adapter_mask, adapter_mask], axis=1)
    pair_bf = adapter_mask_pair.astype(jnp.bfloat16)
    matching_first = ((positions >= 1) & (segment_of(positions - 1, seq_ends) == segment)).astype(
        jnp.float32
    )[:, None]
    matching_second = ((positions >= 2) & (segment_of(positions - 2, seq_ends) == segment)).astype(
        jnp.float32
    )[:, None]
    ahead_one = (segment_of(positions + 1, seq_ends) == segment).astype(jnp.float32)[:, None]
    ahead_two = (segment_of(positions + 2, seq_ends) == segment).astype(jnp.float32)[:, None]
    row_pair = (
        lax.all_gather(packed_in, "tensor", axis=1, tiled=True),
        lax.all_gather(packed_cot, "tensor", axis=1, tiled=True),
    )
    input_complete = row_pair[0].astype(jnp.float32)
    cotangent_half_float = row_pair[1]
    cot_full = cotangent_half_float.astype(jnp.float32)
    mixer_f = mixer_gain.astype(jnp.float32)
    ffn_f = ffn_gain.astype(jnp.float32)
    conv_w = conv_taps.astype(jnp.float32)
    in_full, out_full = fetch_mixer(in_weight, out_weight)
    scale_one = rms_scale(input_complete)
    normalized_rows = (input_complete * scale_one * mixer_f).astype(jnp.bfloat16)
    input_rank_rows = (
        product_simple(normalized_rows, input_adapter_shrink).astype(jnp.bfloat16)
        * adapter_half_float
    )
    projected_rows = jnp.einsum(
        "px,sxa->psa", normalized_rows, in_full, preferred_element_type=jnp.float32
    ) + adapter_scale * jnp.einsum(
        "fw,kwo->fko", input_rank_rows, in_expand, preferred_element_type=jnp.float32
    )
    gate_b = projected_rows[:, 0]
    gate_c = projected_rows[:, 1]
    values_x = projected_rows[:, 2]
    mixed = (gate_b * values_x).astype(jnp.bfloat16)
    prior = shifted(mixed[tok_count - 2 :], "ctx", 1)
    extended = jnp.concatenate([prior, mixed], axis=0).astype(jnp.float32)
    conv_out = (
        conv_w[0] * extended[2:]
        + conv_w[1] * extended[1:-1] * matching_first
        + conv_w[2] * extended[:-2] * matching_second
    )
    gated_rows = (gate_c * conv_out).astype(jnp.bfloat16)
    adapter_branch_sum, output_rank_sum = lax.psum(
        (product_simple(gated_rows, out_full), product_simple(gated_rows, out_shrink)), "tensor"
    )
    output_rank_rows = output_rank_sum.astype(jnp.bfloat16) * adapter_half_float
    hidden_state_rows = input_complete + (
        adapter_branch_sum + adapter_scale * product_simple(output_rank_rows, output_adapter_expand)
    )
    scale_two = rms_scale(hidden_state_rows)
    feedforward_input = (hidden_state_rows * scale_two * ffn_f).astype(jnp.bfloat16)
    feedforward_rank_rows = (
        product_simple(feedforward_input, ffn_shrink).astype(jnp.bfloat16) * pair_bf
    )
    ffn_low_split = feedforward_rank_rows.reshape(tok_count, 2, rank_cols)
    gu_full, down_full = fetch_ffn(gateup_weight, down_weight)
    gate_up_output = jnp.einsum(
        "cm,ame->cae", feedforward_input, gu_full, preferred_element_type=jnp.float32
    ) + adapter_scale * jnp.einsum(
        "vmc,mcb->vmb", ffn_low_split, ffn_expand, preferred_element_type=jnp.float32
    )
    gate_pre = gate_up_output[:, 0]
    up_pre = gate_up_output[:, 1]
    activated_rows = (jax.nn.silu(gate_pre) * up_pre).astype(jnp.bfloat16)
    down_weight_slice = lax.psum_scatter(
        product_simple(activated_rows, down_full).astype(jnp.bfloat16),
        "tensor",
        scatter_dimension=1,
        tiled=True,
    ).astype(jnp.float32)
    down_rank_rows_sum = lax.psum(product_simple(activated_rows, down_shrink), "tensor")
    down_rank_rows = down_rank_rows_sum.astype(jnp.bfloat16) * adapter_half_float
    expand_factor_slice = lax.dynamic_slice_in_dim(
        down_adapter_expand, part_index * half_width, half_width, 1
    )
    hidden_column_slice = lax.dynamic_slice_in_dim(
        hidden_state_rows, part_index * half_width, half_width, 1
    )
    packed_output = (
        hidden_column_slice
        + (down_weight_slice + adapter_scale * product_simple(down_rank_rows, expand_factor_slice))
    ).astype(jnp.bfloat16)
    gu_full, down_full = fetch_ffn(gateup_weight, down_weight)
    down_rank_gradient = (
        adapter_scale * product_backward(cotangent_half_float, down_adapter_expand) * adapter_mask
    ).astype(jnp.bfloat16)
    down_adapter_expand_gradient = adapter_scale * product_leading(
        down_rank_rows, cotangent_half_float
    )
    grad_act = product_backward(cotangent_half_float, down_full) + product_backward(
        down_rank_gradient, down_shrink
    )
    down_shrink_grad = product_leading(activated_rows, down_rank_gradient)
    sigmoid_gate = jax.nn.sigmoid(gate_pre)
    grad_gate = grad_act * up_pre * sigmoid_gate * (1.0 + gate_pre * (1.0 - sigmoid_gate))
    grad_up = grad_act * gate_pre * sigmoid_gate
    grad_gu = jnp.stack([grad_gate, grad_up], axis=1).astype(jnp.bfloat16)
    feedforward_expand_gradient = adapter_scale * jnp.einsum(
        "tje,tjf->jef", ffn_low_split, grad_gu, preferred_element_type=jnp.float32
    )
    feedforward_rank_part = adapter_scale * jnp.einsum(
        "tjf,jef->tje", grad_gu, ffn_expand, preferred_element_type=jnp.float32
    ).reshape(tok_count, 2 * rank_cols)
    ffn_in_part = jnp.einsum("tjf,jdf->td", grad_gu, gu_full, preferred_element_type=jnp.float32)
    ffn_in_sum, ffn_low_sum = lax.psum((ffn_in_part, feedforward_rank_part), "tensor")
    grad_ffn_low = (ffn_low_sum * adapter_mask_pair).astype(jnp.bfloat16)
    grad_ffn_in = ffn_in_sum + product_backward(grad_ffn_low, ffn_shrink)
    ffn_shrink_grad = product_leading(feedforward_input, grad_ffn_low)
    grad_hidden = cot_full + norm_back(hidden_state_rows, scale_two, ffn_f, grad_ffn_in)
    in_full, out_full = fetch_mixer(in_weight, out_weight)
    adapter_branch_gradient = grad_hidden.astype(jnp.bfloat16)
    out_rank_gradient = (
        adapter_scale
        * product_backward(adapter_branch_gradient, output_adapter_expand)
        * adapter_mask
    ).astype(jnp.bfloat16)
    output_expand_gradient = adapter_scale * product_leading(
        output_rank_rows, adapter_branch_gradient
    )
    grad_gated = product_backward(adapter_branch_gradient, out_full) + product_backward(
        out_rank_gradient, out_shrink
    )
    out_shrink_grad = product_leading(gated_rows, out_rank_gradient)
    grad_gate_c = grad_gated * conv_out
    grad_conv = grad_gated * gate_c
    ahead = shifted(grad_conv[:2], "ctx", -1)
    trailing = jnp.concatenate([grad_conv, ahead], axis=0)
    grad_mixed = (
        conv_w[0] * grad_conv
        + conv_w[1] * trailing[1:-1] * ahead_one
        + conv_w[2] * trailing[2:] * ahead_two
    )
    grad_proj = jnp.stack([grad_mixed * values_x, grad_gate_c, grad_mixed * gate_b], axis=1).astype(
        jnp.bfloat16
    )
    input_expand_gradient = adapter_scale * jnp.einsum(
        "te,tjc->jec", input_rank_rows, grad_proj, preferred_element_type=jnp.float32
    )
    input_rank_part = adapter_scale * jnp.einsum(
        "tjc,jec->te", grad_proj, in_expand, preferred_element_type=jnp.float32
    )
    normed_part = jnp.einsum("tjc,jdc->td", grad_proj, in_full, preferred_element_type=jnp.float32)
    normed_sum, input_rank_sum = lax.psum((normed_part, input_rank_part), "tensor")
    in_rank_gradient = (input_rank_sum * adapter_mask).astype(jnp.bfloat16)
    grad_normed = normed_sum + product_backward(in_rank_gradient, input_adapter_shrink)
    in_shrink_grad = product_leading(normalized_rows, in_rank_gradient)
    grad_input_full = grad_hidden + norm_back(input_complete, scale_one, mixer_f, grad_normed)
    packed_grad = lax.dynamic_slice_in_dim(grad_input_full, part_index * half_width, half_width, 1)
    output_blocks = jnp.take(
        packed_output.reshape(group_total, block_rows, half_width), inverse_row, axis=0
    )
    grad_blocks = jnp.take(
        packed_grad.reshape(group_total, block_rows, half_width), inverse_row, axis=0
    )
    block_output = lax.all_to_all(
        output_blocks, "dp", split_axis=0, concat_axis=0, tiled=True
    ).reshape(tok_count, half_width)
    input_grad = (
        lax.all_to_all(
            grad_blocks.astype(jnp.bfloat16), "dp", split_axis=0, concat_axis=0, tiled=True
        )
        .astype(grad_blocks.dtype)
        .reshape(tok_count, half_width)
    )
    totals = lax.psum(
        (
            in_shrink_grad,
            input_expand_gradient,
            out_shrink_grad,
            output_expand_gradient,
            ffn_shrink_grad,
            feedforward_expand_gradient,
            down_shrink_grad,
            down_adapter_expand_gradient,
        ),
        ("dp", "ctx"),
    )
    return (
        block_output,
        input_grad,
        totals[0],
        totals[1],
        totals[2],
        totals[3],
        totals[4],
        totals[5],
        totals[6],
        totals[7],
    )


def solution(mesh):
    placed = (
        P(("dp", "ctx"), "tensor"),
        P(("dp", "ctx"), "tensor"),
        P("dp", None),
        P("dp"),
        P("dp"),
        P(),
        P(),
        P(None, "tensor"),
        P(None, "dp", "tensor"),
        P("tensor", "dp"),
        P(None, "dp", "tensor"),
        P("tensor", "dp"),
        P(),
        P(None, None, "tensor"),
        P("tensor", None),
        P(),
        P(),
        P(None, None, "tensor"),
        P("tensor", None),
        P(),
    )
    return jax.shard_map(
        body,
        mesh=mesh,
        in_specs=placed,
        out_specs=(
            P(("dp", "ctx"), "tensor"),
            P(("dp", "ctx"), "tensor"),
            P(),
            P(None, None, "tensor"),
            P("tensor", None),
            P(),
            P(),
            P(None, None, "tensor"),
            P("tensor", None),
            P(),
        ),
        check_vma=False,
    )
```

profile of v0, /device:TPU:0, one launch (start us, length us, event | category | flops | bytes accessed | tf_op | source)
XLA Modules:
  0.0 1380.1 jit_solution(14482190222094816660)
XLA Ops:
  7.2 25.2 %all_to_all.20 = bf16[4,192,1024]{2,1,0:T(8,128)(2,1)} all-to-all(bf16[4,192,1024]{2,1,0:T(8,128)(2,1)} %bitcast.155), channel_id=1, replica_groups=mesh['dp'=4,'ctx'=4,'tensor'=2] {'dp'}, dimensions={0} | all-to-all | bytes 3145728 | tf_op jit(solution)/shard_map/all_to_all | solution.py:95
  39.3 16.7 %all-to-all-done.2 = bf16[4,192,1024]{2,1,0:T(8,128)(2,1)S(1)} async-done(((bf16[4,192,1024]{2,1,0:T(8,128)(2,1)}), bf16[4,192,1024]{2,1,0:T(8,128)(2,1)S(1)}, u32[]{:S(2)}, u32[]{:S(2)}) %all-to-all-start.2) | async-done | bytes 1572896 | tf_op jit(solution)/shard_map/all_to_all | solution.py:102
  65.6 42.4 %all-gather.7.cloned.1.call-done = bf16[768,2048]{1,0:T(8,128)(2,1)} async-done(((bf16[768,1024]{1,0:T(8,128)(2,1)}), bf16[768,2048]{1,0:T(8,128)(2,1)}) %all-gather.7.cloned.1.call-update) | async-done | bytes 3145744 | tf_op jit(solution)/shard_map/all_gather | solution.py:133
  111.9 79.8 %all-gather.9.cloned.1.call-done = bf16[3,2048,1024]{2,1,0:T(8,128)(2,1)} async-done(((bf16[3,512,1024]{2,1,0:T(8,128)(2,1)}), bf16[3,2048,1024]{2,1,0:T(8,128)(2,1)}) %all-gather.9.cloned.1.call-update) | async-done | bytes 12582928 | tf_op jit(solution)/shard_map/all_gather | solution.py:49
  191.7 13.6 fusion.17
  215.4 12.4 all-gather.11.cloned.1.call-done
  227.8 7.4 fusion.72
  237.9 36.9 %all-gather.17.cloned.1.call-done = bf16[768,2048]{1,0:T(8,128)(2,1)} async-done(((bf16[768,1024]{1,0:T(8,128)(2,1)}), bf16[768,2048]{1,0:T(8,128)(2,1)}) %all-gather.17.cloned.1.call-update) | async-done | bytes 3145744 | tf_op jit(solution)/shard_map/all_gather | solution.py:134
  278.3 74.0 %all-gather.15.cloned.1.call-done = bf16[2816,2048]{1,0:T(8,128)(2,1)} async-done(((bf16[2816,512]{1,0:T(8,128)(2,1)}), bf16[2816,2048]{1,0:T(8,128)(2,1)}) %all-gather.15.cloned.1.call-update) | async-done | bytes 11534352 | tf_op jit(solution)/shard_map/all_gather | solution.py:57
  352.3 15.8 %fusion.75 = f32[768,2816]{1,0:T(8,128)} fusion(bf16[768,2048]{1,0:T(8,128)(2,1)} %all-gather.17.cloned.1.call-done, bf16[2816,2048]{1,0:T(8,128)(2,1)} %all-gather.15.cloned.1.call-done), kind=kOutput, calls=%fused_computation.166 | convolution fusion | flops 8858370048 | bytes 23330816 | tf_op jit(solution)/shard_map/dot_general | solution.py:32
  369.5 25.5 %all-reduce.17 = bf16[768,128]{1,0:T(8,128)(2,1)S(1)} all-reduce(f32[768,128]{1,0:T(8,128)} %fusion.73), channel_id=1, replica_groups=mesh['dp'=4,'ctx'=4,'tensor'=2] {'tensor'}, use_global_device_ids=true, to_apply=%region_7.9 | all-reduce | flops 98304 | bytes 589824 | tf_op jit(solution)/shard_map/psum | solution.py:166
  395.0 121.3 %all-reduce.10.cloned.1.call-done = f32[768,2048]{1,0:T(8,128)} async-done(((f32[768,2048]{1,0:T(8,128)}), f32[768,2048]{1,0:T(8,128)}) %all-reduce.10.cloned.1.call-update) | async-done | bytes 6291472 | tf_op jit(solution)/shard_map/psum | solution.py:166
  528.2 131.7 %all-gather.13.cloned.1.call-done = bf16[2,2048,2816]{2,1,0:T(8,128)(2,1)} async-done(((bf16[2,512,2816]{2,1,0:T(8,128)(2,1)}), bf16[2,2048,2816]{2,1,0:T(8,128)(2,1)}) %all-gather.13.cloned.1.call-update) | async-done | bytes 23068688 | tf_op jit(solution)/shard_map/all_gather | solution.py:56
  659.9 23.8 %fusion.15 = f32[768,2,2816]{2,0,1:T(8,128)S(1)} fusion(bf16[2,2048,2816]{2,1,0:T(8,128)(2,1)} %all-gather.13.cloned.1.call-done, bf16[768,2048]{1,0:T(8,128)(2,1)} %copy-done.11), kind=kOutput, calls=%fused_computation.57 | convolution fusion | flops 17716740096 | bytes 43515904 | tf_op jit(solution)/shard_map/cm,ame->cae/dot_general | solution.py:180
  683.6 9.4 bitcast_add_fusion
  693.0 13.5 fusion.2
  713.6 25.4 %convolution_bitcast_fusion.1 = f32[768,2048]{1,0:T(8,128)} fusion(bf16[2,2048,2816]{2,1,0:T(8,128)(2,1)} %all-gather.13.cloned.1.call-done, bf16[768,1,2816]{2,0,1:T(8,128)(2,1)} %get-tuple-element.53, bf16[768,1,2816]{2,0,1:T(8,128)(2,1)} %copy-done.65), kind=kOutput, calls=%fused_computation.31 | convolution fusion | flops 17721065472 | bytes 38010880 | tf_op jit(solution)/shard_map/tjf,jdf->td/dot_general | solution.py:227
  739.0 14.4 %convolution_convert_fusion = bf16[768,2048]{1,0:T(8,128)(2,1)} fusion(bf16[768,2816]{1,0:T(8,128)(2,1)} %get-tuple-element.54, bf16[2816,2048]{1,0:T(8,128)(2,1)} %all-gather.15.cloned.1.call-done), kind=kOutput, calls=%fused_computation.32 | convolution fusion | flops 8859942912 | bytes 19005440 | tf_op jit(solution)/shard_map/dot_general | solution.py:28
  753.6 156.1 %all-reduce.16.cloned.1.call-done = (f32[768,2048]{1,0:T(8,128)}, f32[768,256]{1,0:T(8,128)}) async-done(((f32[768,2048]{1,0:T(8,128)}, f32[768,256]{1,0:T(8,128)}), (f32[768,2048]{1,0:T(8,128)}, f32[768,256]{1,0:T(8,128)})) %all-reduce.16.cloned.1.call-update) | async-done | bytes 7077904 | tf_op jit(solution)/shard_map/psum | solution.py:228
  940.3 14.7 %convolution_bitcast_fusion = f32[768,2048]{1,0:T(8,128)} fusion(bf16[3,2048,1024]{2,1,0:T(8,128)(2,1)} %all-gather.9.cloned.1.call-done, bf16[768,1,1024]{2,0,1:T(8,128)(2,1)S(1)} %fusion.23, bf16[768,1,1024]{2,0,1:T(8,128)(2,1)S(1)} %get-tuple-element.57, bf16[768,1,1024]{2,0,1:T(8,128)(2,1)S(1)} %get-tuple-element.48), kind=kOutput, calls=%fused_computation.30 | convolution fusion | flops 9668395008 | bytes 23592960 | tf_op jit(solution)/shard_map/tjc,jdc->td/dot_general | solution.py:265
  978.8 41.3 %all-reduce.18 = (bf16[768,128]{1,0:T(8,128)(2,1)S(1)}, bf16[768,128]{1,0:T(8,128)(2,1)S(1)}) all-reduce(f32[768,128]{1,0:T(8,128)S(1)} %fusion.74, f32[768,128]{1,0:T(8,128)S(1)} %fusion.27), channel_id=1, replica_groups=mesh['dp'=4,'ctx'=4,'tensor'=2] {'tensor'}, use_global_device_ids=true, to_apply=%region_10.12 | all-reduce | flops 196608 | bytes 1179648 | tf_op jit(solution)/shard_map/psum | solution.py:194
  1035.0 92.8 %all-reduce.12.cloned.1.call-done = f32[768,2048]{1,0:T(8,128)} async-done(((f32[768,2048]{1,0:T(8,128)}), f32[768,2048]{1,0:T(8,128)}) %all-reduce.12.cloned.1.call-update) | async-done | bytes 6291472 | tf_op jit(solution)/shard_map/psum | solution.py:266
  1141.1 39.8 %all_to_all.21 = bf16[4,192,1024]{2,1,0:T(8,128)(2,1)S(1)} all-to-all(bf16[4,192,1024]{2,1,0:T(8,128)(2,1)S(1)} %get-tuple-element.67), channel_id=1, replica_groups=mesh['dp'=4,'ctx'=4,'tensor'=2] {'dp'}, dimensions={0} | all-to-all | bytes 3145728 | tf_op jit(solution)/shard_map/all_to_all | solution.py:278
  1185.3 170.9 %all-reduce.14.cloned.1.call-done = (f32[2048,128]{1,0:T(8,128)}, f32[3,128,1024]{1,2,0:T(8,128)}, f32[1024,128]{1,0:T(8,128)}, f32[128,2048]{1,0:T(8,128)}, f32...) async-done(((f32[2048,128]{1,0:T(8,128)}, f32[3,128,1024]{1,2,0:T(8,128)}, f32[1024,128]{1,0:T(8,128)}, ...) | async-done | bytes 11665424 | tf_op jit(solution)/shard_map/psum | solution.py:288
  (258 shorter events, 159.8 us)
Async XLA Ops:
  7.2 676.5 %copy-start = (bf16[2,128,2816]{2,1,0:T(8,128)(2,1)S(1)}, bf16[2,128,2816]{2,1,0:T(8,128)(2,1)}, u32[]{:S(2)}) copy-start(bf16[2,128,2816]{2,1,0:T(8,128)(2,1)} %param.39) | copy-start | bytes 4325380
  32.4 23.6 %all-to-all-start.2 = ((bf16[4,192,1024]{2,1,0:T(8,128)(2,1)}), bf16[4,192,1024]{2,1,0:T(8,128)(2,1)S(1)}, u32[]{:S(2)}, u32[]{:S(2)}) async-start(bf16[4,192,1024]{2,1,0:T(8,128)(2,1)} %bitcast.156), calls=%async_computation.3 | async-start | bytes 3145728 | tf_op jit(solution)/shard_map/all_to_all | solution.py:102
  36.0 72.0 %all-gather.7.cloned.1.call-start = ((), (), s32[]{:S(2)}) async-start(), calls=%async_computation.5 | async-start | bytes 4718592 | tf_op jit(solution)/shard_map/all_gather | solution.py:133
  61.8 130.0 %all-gather.9.cloned.1.call-start = ((), (), s32[]{:S(2)}) async-start(), calls=%async_computation.6 | async-start | bytes 15728640 | tf_op jit(solution)/shard_map/all_gather | solution.py:49
  62.6 165.3 %all-gather.11.cloned.1.call-start = ((), (), s32[]{:S(2)}) async-start(), calls=%async_computation.7 | async-start | bytes 5242880 | tf_op jit(solution)/shard_map/all_gather | solution.py:50
  63.3 211.5 %all-gather.17.cloned.1.call-start = ((), (), s32[]{:S(2)}) async-start(), calls=%async_computation.12 | async-start | bytes 4718592 | tf_op jit(solution)/shard_map/all_gather | solution.py:134
  63.9 288.5 %all-gather.15.cloned.1.call-start = ((), (), s32[]{:S(2)}) async-start(), calls=%async_computation.10 | async-start | bytes 14417920 | tf_op jit(solution)/shard_map/all_gather | solution.py:57
  64.5 451.9 %all-reduce.10.cloned.1.call-start = ((), (), s32[]{:S(2)}) async-start(), calls=%async_computation.8 | async-start | bytes 12582912 | tf_op jit(solution)/shard_map/psum | solution.py:166
  64.5 127.2 %copy-start.54 = (f32[2048]{0:T(1024)}, f32[2048]{0:T(1024)S(1)}, u32[]{:S(2)}) copy-start(f32[2048]{0:T(1024)S(1)} %convert_element_type.128) | copy-start | bytes 24580
  111.9 93.4 %copy-start.41 = (bf16[768,128,1]{1,0,2:T(8,128)(2,1)}, bf16[768,128,1]{1,0,2:T(8,128)(2,1)S(1)}, u32[]{:S(2)}) copy-start(bf16[768,128,1]{1,0,2:T(8,128)(2,1)S(1)} %fusion.32) | copy-start | bytes 589828
  207.3 4.7 collective-permute-start
  215.4 152.8 %copy-start.7 = (bf16[768,1024]{1,0:T(8,128)(2,1)}, bf16[768,1024]{1,0:T(8,128)(2,1)S(1)}, u32[]{:S(2)}) copy-start(bf16[768,1024]{1,0:T(8,128)(2,1)S(1)} %get-tuple-element.50) | copy-start | bytes 4718596
  235.2 424.6 %all-gather.13.cloned.1.call-start = ((), (), s32[]{:S(2)}) async-start(), calls=%async_computation.9 | async-start | bytes 28835840 | tf_op jit(solution)/shard_map/all_gather | solution.py:56
  236.0 673.7 %all-reduce.16.cloned.1.call-start = ((), (), s32[]{:S(2)}) async-start(), calls=%async_computation.15 | async-start | bytes 14155776 | tf_op jit(solution)/shard_map/psum | solution.py:228
  368.2 148.1 %copy-start.14 = (bf16[128,2048]{1,0:T(8,128)(2,1)S(1)}, bf16[128,2048]{1,0:T(8,128)(2,1)}, u32[]{:S(2)}) copy-start(bf16[128,2048]{1,0:T(8,128)(2,1)} %param.37) | copy-start | bytes 1572868
  395.0 126.0 %copy-start.16 = (bf16[768,128]{1,0:T(8,128)(2,1)}, bf16[768,128]{1,0:T(8,128)(2,1)S(1)}, u32[]{:S(2)}) copy-start(bf16[768,128]{1,0:T(8,128)(2,1)S(1)} %all-reduce.17) | copy-start | bytes 589828
  739.0 290.9 %reduce-scatter.2.cloned.1.call-start = ((), (), s32[]{:S(2)}) async-start(), calls=%async_computation.11 | async-start | bytes 4718592 | tf_op jit(solution)/shard_map/reduce_scatter | solution.py:188
  753.5 156.2 %copy-start.26 = (f32[768,128]{1,0:T(8,128)S(1)}, f32[768,128]{1,0:T(8,128)}, u32[]{:S(2)}) copy-start(f32[768,128]{1,0:T(8,128)} %compare_convert_fusion) | copy-start | bytes 1179652
  753.5 156.2 %copy-start.31 = (bf16[2048,256]{1,0:T(8,128)(2,1)S(1)}, bf16[2048,256]{1,0:T(8,128)(2,1)}, u32[]{:S(2)}) copy-start(bf16[2048,256]{1,0:T(8,128)(2,1)} %param.38) | copy-start | bytes 3145732
  753.5 374.3 %all-reduce.12.cloned.1.call-start = ((), (), s32[]{:S(2)}) async-start(), calls=%async_computation.13 | async-start | bytes 12582912 | tf_op jit(solution)/shard_map/psum | solution.py:266
  929.3 5.5 collective-permute-start.1
  955.0 401.1 %all-reduce.14.cloned.1.call-start = ((), (), s32[]{:S(2)}) async-start(), calls=%async_computation.14 | async-start | bytes 23330816 | tf_op jit(solution)/shard_map/psum | solution.py:288
  1033.2 94.6 %copy-start.39 = (bf16[2048,128]{1,0:T(8,128)(2,1)S(1)}, bf16[2048,128]{1,0:T(8,128)(2,1)}, u32[]{:S(2)}) copy-start(bf16[2048,128]{1,0:T(8,128)(2,1)} %param.34) | copy-start | bytes 1572868
  1180.9 178.3 %all-to-all-start.3 = ((bf16[4,192,1024]{2,1,0:T(8,128)(2,1)}), bf16[4,192,1024]{2,1,0:T(8,128)(2,1)}, u32[]{:S(2)}, u32[]{:S(2)}) async-start(bf16[4,192,1024]{2,1,0:T(8,128)(2,1)} %get-tuple-element.66), calls=%async_computation.4 | async-start | bytes 3145728 | tf_op jit(solution)/shard_map/all_to_all | solution.py:282
  (64 other events, 636.3 us)
Sparse Core Ops, SparseCore 0:
  61.9 46.0 all-gather.6
  109.6 82.0 all-gather.8
  193.3 34.4 all-gather.10
  229.8 44.9 all-gather.16
  276.2 76.1 all-gather.14
  354.6 161.6 all-reduce.9
  518.0 141.8 all-gather.12
  739.1 170.5 all-reduce.15
  911.9 43.3 reduce-scatter.1
  957.7 170.0 all-reduce.11
  1133.8 222.3 all-reduce.13
where the time goes:
time: 1390 us; the launch traced here: 1380 us
  waiting for transfers between devices  944 us (68%)
  matrix products  208 us (15%)
  blocking collectives  132 us (9%)
  local copies, waits for them, and re-layouts  36.4 us (3%)
  other arithmetic  31.6 us (2%)
  between operations  15.3 us (1%)
    psum x1, waiting for transfers between devices, body(): lax.psum((in_shrink_grad, input_expand_gradient, out_shrink_grad, output_...  171 us
    psum x1, waiting for transfers between devices, body(): lax.psum((ffn_in_part, feedforward_rank_part), 'tensor')  156 us
    all_gather x1, waiting for transfers between devices, fetch_ffn(): lax.all_gather(gateup_weight, 'dp', axis=1, tiled=True)  132 us
    psum x1, waiting for transfers between devices, body(): lax.psum((product_simple(gated_rows, out_full), product_simple(gated_rows...  121 us
    psum x1, waiting for transfers between devices, body(): lax.psum((normed_part, input_rank_part), 'tensor')  92.8 us
    all_gather x1, waiting for transfers between devices, fetch_mixer(): lax.all_gather(in_weight, 'dp', axis=1, tiled=True)  79.8 us
    all_gather x1, waiting for transfers between devices, fetch_ffn(): lax.all_gather(down_weight, 'dp', axis=1, tiled=True)  74 us
    dot_general x8, matrix products, product_backward(): lax.dot_general(left, right, (((1,), (1,)), ((), ())), preferred_element_...  49.3 us
  transfers between devices with their start and end apart: 15, of which 13 were waited for; matrix products, arithmetic and copies ran while one was open for 12% of the time, Pallas kernels for 0%

commit v1 on v0

--- a/solution.py
+++ b/solution.py
@@ -52,8 +52,23 @@
 
 
 def fetch_ffn(gateup_weight, down_weight):
+
+    def lay_the_record(load, chip_axis, dim_i):
+        res, new, clean = (lax.axis_size(chip_axis), lax.axis_index(chip_axis), load.shape[dim_i])
+        chunks = list(map(lambda kk: (kk, (kk + 1) % res), range(res)))
+        z2 = load
+        top = jnp.zeros((*load.shape[:dim_i], res * clean, *load.shape[dim_i + 1 :]), load.dtype)
+        at = 0
+        while at < res:
+            s_next = (new - at) % res
+            top = lax.dynamic_update_slice_in_dim(top, z2, s_next * clean, axis=dim_i)
+            if at < res - 1:
+                z2 = lax.ppermute(z2, chip_axis, chunks)
+            at += 1
+        return top
+
     return (
-        lax.all_gather(gateup_weight, "dp", axis=1, tiled=True),
+        lay_the_record(gateup_weight, "dp", 1),
         lax.all_gather(down_weight, "dp", axis=1, tiled=True),
     )
 

time: 1390 us -> 1320 us (0.950)
  waiting for transfers between devices: 944 us -> 827 us
  local copies, waits for them, and re-layouts: 36.4 us -> 70.6 us
    ppermute x0 -> x3, waiting for transfers between devices: none -> 235 us  [lay_the_record(): z2 = lax.ppermute(z2, chip_axis, chunks)]
    all_gather x1 -> x0, waiting for transfers between devices: 132 us -> none  [fetch_ffn(): lax.all_gather(gateup_weight, 'dp', axis=1, tiled=True)]
    all_gather x1, waiting for transfers between devices: 79.8 us -> 0.01 us  [fetch_mixer(): lax.all_gather(in_weight, 'dp', axis=1, tiled=True)]
    all_gather x1, waiting for transfers between devices: 74 us -> 29.7 us  [fetch_ffn(): lax.all_gather(down_weight, 'dp', axis=1, tiled=True)]
    all_gather x1, waiting for transfers between devices: 42.4 us -> 0.01 us  [body(): lax.all_gather(packed_in, 'tensor', axis=1, tiled=True)]
    all_gather x1, waiting for transfers between devices: 36.9 us -> 0.01 us  [body(): lax.all_gather(packed_cot, 'tensor', axis=1, tiled=True)]
    dynamic_update_slice x0 -> x4, local copies, waits for them, and re-layouts: none -> 23.2 us  [lay_the_record(): top = lax.dynamic_update_slice_in_dim(top, z2, s_next * clean, axis=dim_i)]
    unnamed x155 -> x183, local copies, waits for them, and re-layouts: 25.7 us -> 29.1 us
  transfers between devices with their start and end apart: 15 -> 17, of which waited for: 13 -> 11; matrix products, arithmetic and copies ran while one was open for 12% -> 15% of each run, Pallas kernels for 0% -> 0%
where the time goes in v1:
time: 1320 us; the launch traced here: 1310 us
  waiting for transfers between devices  827 us (63%)
  matrix products  219 us (17%)
  blocking collectives  132 us (10%)
  local copies, waits for them, and re-layouts  70.6 us (5%)
  other arithmetic  34.7 us (3%)
  between operations  15.9 us (1%)
  starting transfers between devices  14.5 us (1%)
    ppermute x3, waiting for transfers between devices, lay_the_record(): z2 = lax.ppermute(z2, chip_axis, chunks)  235 us
    psum x1, waiting for transfers between devices, body(): lax.psum((in_shrink_grad, input_expand_gradient, out_shrink_grad, output_...  171 us
    psum x1, waiting for transfers between devices, body(): lax.psum((ffn_in_part, feedforward_rank_part), 'tensor')  156 us
    psum x1, waiting for transfers between devices, body(): lax.psum((product_simple(gated_rows, out_full), product_simple(gated_rows...  121 us
    psum x1, waiting for transfers between devices, body(): lax.psum((normed_part, input_rank_part), 'tensor')  89.9 us
    dot_general x8, matrix products, product_backward(): lax.dot_general(left, right, (((1,), (1,)), ((), ())), preferred_element_...  55.9 us
    psum x1, blocking collectives, body(): lax.psum(product_simple(activated_rows, down_shrink), 'tensor')  40.4 us
    all_to_all x1, blocking collectives, body(): lax.all_to_all(output_blocks, 'dp', split_axis=0, concat_axis=0, tiled=True)  39.8 us
  transfers between devices with their start and end apart: 17, of which 11 were waited for; matrix products, arithmetic and copies ran while one was open for 15% of the time, Pallas kernels for 0%

profile of v1, /device:TPU:0, one launch (start us, length us, event | category | flops | bytes accessed | tf_op | source)
XLA Modules:
  0.0 1313.2 jit_solution(13714668586375870277)
XLA Ops:
  7.2 25.3 %all_to_all.20 = bf16[4,192,1024]{2,1,0:T(8,128)(2,1)} all-to-all(bf16[4,192,1024]{2,1,0:T(8,128)(2,1)} %bitcast.155), channel_id=1, replica_groups=mesh['dp'=4,'ctx'=4,'tensor'=2] {'dp'}, dimensions={0} | all-to-all | bytes 3145728 | tf_op jit(solution)/shard_map/all_to_all | solution.py:110
  39.3 16.8 %all-to-all-done.2 = bf16[4,192,1024]{2,1,0:T(8,128)(2,1)S(1)} async-done(((bf16[4,192,1024]{2,1,0:T(8,128)(2,1)}), bf16[4,192,1024]{2,1,0:T(8,128)(2,1)S(1)}, u32[]{:S(2)}, u32[]{:S(2)}) %all-to-all-start.2) | async-done | bytes 1572896 | tf_op jit(solution)/shard_map/all_to_all | solution.py:117
  64.6 79.4 %collective-permute-done.1 = bf16[2,512,2816]{2,1,0:T(8,128)(2,1)} collective-permute-done((bf16[2,512,2816]{2,1,0:T(8,128)(2,1)}, bf16[2,512,2816]{2,1,0:T(8,128)(2,1)}, u32[]{:S(2)}, u32[]{:S(2)}) %collective-permute-start.1) | collective-permute-done | bytes 5767200 | tf_op jit(solution)/shard_map/ppermute | solution.py:66
  151.6 129.7 %collective-permute-done.2 = bf16[2,512,2816]{2,1,0:T(8,128)(2,1)} collective-permute-done((bf16[2,512,2816]{2,1,0:T(8,128)(2,1)}, bf16[2,512,2816]{2,1,0:T(8,128)(2,1)}, u32[]{:S(2)}, u32[]{:S(2)}) %collective-permute-start.2) | collective-permute-done | bytes 5767200 | tf_op jit(solution)/shard_map/ppermute | solution.py:66
  281.4 14.2 %fusion.16 = f32[768,3,1024]{2,0,1:T(8,128)S(1)} fusion(bf16[3,2048,1024]{2,1,0:T(8,128)(2,1)} %all-gather.8.cloned.1.call-done, f32[2048]{0:T(1024)S(1)} %convert_element_type.128, f32[768]{0:T(1024)S(1)} %add_rsqrt_fusion.1, bf16[768,2048]{1,0:T(8,128)(2,1)} %all-gather.6.cloned.1.call-done), kind=kOutput, calls=%fused_computation.58 | convolution fusion | flops 9669967872 | bytes 25177088 | tf_op jit(solution)/shard_map/px,sxa->psa/dot_general | solution.py:164
  311.3 8.0 fusion.72
  319.6 8.5 broadcast.215
  349.4 25.6 %collective-permute-done.3 = bf16[2,512,2816]{2,1,0:T(8,128)(2,1)} collective-permute-done((bf16[2,512,2816]{2,1,0:T(8,128)(2,1)}, bf16[2,512,2816]{2,1,0:T(8,128)(2,1)}, u32[]{:S(2)}, u32[]{:S(2)}) %collective-permute-start.3) | collective-permute-done | bytes 5767200 | tf_op jit(solution)/shard_map/ppermute | solution.py:66
  380.4 29.7 %all-gather.12.cloned.1.call-done = bf16[2816,2048]{1,0:T(8,128)(2,1)} async-done(((bf16[2816,512]{1,0:T(8,128)(2,1)}), bf16[2816,2048]{1,0:T(8,128)(2,1)}) %all-gather.12.cloned.1.call-update) | async-done | bytes 11534352 | tf_op jit(solution)/shard_map/all_gather | solution.py:72
  410.1 15.9 %fusion.76 = f32[768,2816]{1,0:T(8,128)} fusion(bf16[768,2048]{1,0:T(8,128)(2,1)} %all-gather.14.cloned.1.call-done, bf16[2816,2048]{1,0:T(8,128)(2,1)} %all-gather.12.cloned.1.call-done), kind=kOutput, calls=%fused_computation.171 | convolution fusion | flops 8858370048 | bytes 23330816 | tf_op jit(solution)/shard_map/dot_general | solution.py:32
  427.3 26.8 %all-reduce.17 = bf16[768,128]{1,0:T(8,128)(2,1)S(1)} all-reduce(f32[768,128]{1,0:T(8,128)} %fusion.73), channel_id=1, replica_groups=mesh['dp'=4,'ctx'=4,'tensor'=2] {'tensor'}, use_global_device_ids=true, to_apply=%region_7.9 | all-reduce | flops 98304 | bytes 589824 | tf_op jit(solution)/shard_map/psum | solution.py:181
  454.1 121.1 %all-reduce.10.cloned.1.call-done = f32[768,2048]{1,0:T(8,128)} async-done(((f32[768,2048]{1,0:T(8,128)}), f32[768,2048]{1,0:T(8,128)}) %all-reduce.10.cloned.1.call-update) | async-done | bytes 6291472 | tf_op jit(solution)/shard_map/psum | solution.py:181
  585.4 8.3 fusion.74
  593.8 26.8 %bitcast_add_fusion = f32[768,2,2816]{2,0,1:T(8,128)} fusion(f32[2,768,2816]{2,1,0:T(8,128)} %fusion.74, bf16[2,2048,2816]{2,1,0:T(8,128)(2,1)} %constant_dynamic-update-slice_fusion, bf16[768,2048]{1,0:T(8,128)(2,1)S(1)} %copy-done.11), kind=kOutput, calls=%fused_computation.4 | convolution fusion | flops 17725390848 | bytes 60817408 | tf_op jit(solution)/shard_map/cm,ame->cae/dot_general | solution.py:195
  620.6 14.5 %fusion.2 = (bf16[768,1,2816]{2,0,1:T(8,128)(2,1)S(1)}, bf16[768,1,2816]{2,0,1:T(8,128)(2,1)}, bf16[768,2816]{1,0:T(8,128)(2,1)}) fusion(f32[768,2,2816]{2,0,1:T(8,128)} %bitcast_add_fusion, f32[768,2816]{1,0:T(8,128)} %fusion.76, bf16[768,128]{1,0:T(8,128)(2,1)S(1)} %copy-done.48, bf16[2816,128]{1,0:T(8,128)(2,1)S(1)} %copy-done.40), kind=kOutput, calls=%fused_computation.28 | convolution fusion | flops 590413824 | bytes 39845888 | tf_op jit(solution)/shard_map/dot_general | solution.py:32
  640.9 24.0 %convolution_bitcast_fusion.1 = f32[768,2048]{1,0:T(8,128)} fusion(bf16[2,2048,2816]{2,1,0:T(8,128)(2,1)} %constant_dynamic-update-slice_fusion, bf16[768,1,2816]{2,0,1:T(8,128)(2,1)} %get-tuple-element.53, bf16[768,1,2816]{2,0,1:T(8,128)(2,1)S(1)} %get-tuple-element.52), kind=kOutput, calls=%fused_computation.31 | convolution fusion | flops 17721065472 | bytes 38010880 | tf_op jit(solution)/shard_map/tjf,jdf->td/dot_general | solution.py:242
  666.1 14.4 %convolution_convert_fusion = bf16[768,2048]{1,0:T(8,128)(2,1)} fusion(bf16[768,2816]{1,0:T(8,128)(2,1)} %get-tuple-element.54, bf16[2816,2048]{1,0:T(8,128)(2,1)} %all-gather.12.cloned.1.call-done), kind=kOutput, calls=%fused_computation.32 | convolution fusion | flops 8859942912 | bytes 19005440 | tf_op jit(solution)/shard_map/dot_general | solution.py:28
  680.6 156.1 %all-reduce.16.cloned.1.call-done = (f32[768,2048]{1,0:T(8,128)}, f32[768,256]{1,0:T(8,128)}) async-done(((f32[768,2048]{1,0:T(8,128)}, f32[768,256]{1,0:T(8,128)}), (f32[768,2048]{1,0:T(8,128)}, f32[768,256]{1,0:T(8,128)})) %all-reduce.16.cloned.1.call-update) | async-done | bytes 7077904 | tf_op jit(solution)/shard_map/psum | solution.py:243
  836.8 9.6 multiply_reduce_fusion.1
  876.6 14.7 %convolution_bitcast_fusion = f32[768,2048]{1,0:T(8,128)} fusion(bf16[3,2048,1024]{2,1,0:T(8,128)(2,1)} %all-gather.8.cloned.1.call-done, bf16[768,1,1024]{2,0,1:T(8,128)(2,1)S(1)} %fusion.22, bf16[768,1,1024]{2,0,1:T(8,128)(2,1)S(1)} %get-tuple-element.57, bf16[768,1,1024]{2,0,1:T(8,128)(2,1)S(1)} %get-tuple-element.48), kind=kOutput, calls=%fused_computation.30 | convolution fusion | flops 9668395008 | bytes 23592960 | tf_op jit(solution)/shard_map/tjc,jdc->td/dot_general | solution.py:280
  915.7 40.4 %all-reduce.18 = (bf16[768,128]{1,0:T(8,128)(2,1)S(1)}, bf16[768,128]{1,0:T(8,128)(2,1)S(1)}) all-reduce(f32[768,128]{1,0:T(8,128)S(1)} %fusion.75, f32[768,128]{1,0:T(8,128)S(1)} %fusion.26), channel_id=1, replica_groups=mesh['dp'=4,'ctx'=4,'tensor'=2] {'tensor'}, use_global_device_ids=true, to_apply=%region_10.12 | all-reduce | flops 196608 | bytes 1179648 | tf_op jit(solution)/shard_map/psum | solution.py:209
  971.1 89.9 %all-reduce.12.cloned.1.call-done = f32[768,2048]{1,0:T(8,128)} async-done(((f32[768,2048]{1,0:T(8,128)}), f32[768,2048]{1,0:T(8,128)}) %all-reduce.12.cloned.1.call-update) | async-done | bytes 6291472 | tf_op jit(solution)/shard_map/psum | solution.py:281
  1074.3 39.8 %all_to_all.21 = bf16[4,192,1024]{2,1,0:T(8,128)(2,1)S(1)} all-to-all(bf16[4,192,1024]{2,1,0:T(8,128)(2,1)S(1)} %get-tuple-element.67), channel_id=1, replica_groups=mesh['dp'=4,'ctx'=4,'tensor'=2] {'dp'}, dimensions={0} | all-to-all | bytes 3145728 | tf_op jit(solution)/shard_map/all_to_all | solution.py:293
  1118.4 170.5 %all-reduce.14.cloned.1.call-done = (f32[2048,128]{1,0:T(8,128)}, f32[3,128,1024]{1,2,0:T(8,128)}, f32[1024,128]{1,0:T(8,128)}, f32[128,2048]{1,0:T(8,128)}, f32...) async-done(((f32[2048,128]{1,0:T(8,128)}, f32[3,128,1024]{1,2,0:T(8,128)}, f32[1024,128]{1,0:T(8,128)}, ...) | async-done | bytes 11665424 | tf_op jit(solution)/shard_map/psum | solution.py:303
  (295 shorter events, 187.5 us)
Async XLA Ops:
  7.2 578.3 %copy-start = (bf16[2,128,2816]{2,1,0:T(8,128)(2,1)S(1)}, bf16[2,128,2816]{2,1,0:T(8,128)(2,1)}, u32[]{:S(2)}) copy-start(bf16[2,128,2816]{2,1,0:T(8,128)(2,1)} %param.39) | copy-start | bytes 4325380
  32.5 23.6 %all-to-all-start.2 = ((bf16[4,192,1024]{2,1,0:T(8,128)(2,1)}), bf16[4,192,1024]{2,1,0:T(8,128)(2,1)S(1)}, u32[]{:S(2)}, u32[]{:S(2)}) async-start(bf16[4,192,1024]{2,1,0:T(8,128)(2,1)} %bitcast.156), calls=%async_computation.3 | async-start | bytes 3145728 | tf_op jit(solution)/shard_map/all_to_all | solution.py:117
  36.0 110.0 %all-gather.6.cloned.1.call-start = ((), (), s32[]{:S(2)}) async-start(), calls=%async_computation.5 | async-start | bytes 4718592 | tf_op jit(solution)/shard_map/all_gather | solution.py:148
  61.8 219.6 %all-gather.8.cloned.1.call-start = ((), (), s32[]{:S(2)}) async-start(), calls=%async_computation.6 | async-start | bytes 15728640 | tf_op jit(solution)/shard_map/all_gather | solution.py:49
  62.6 248.7 %all-gather.10.cloned.1.call-start = ((), (), s32[]{:S(2)}) async-start(), calls=%async_computation.7 | async-start | bytes 5242880 | tf_op jit(solution)/shard_map/all_gather | solution.py:50
  63.3 271.2 %all-gather.14.cloned.1.call-start = ((), (), s32[]{:S(2)}) async-start(), calls=%async_computation.11 | async-start | bytes 4718592 | tf_op jit(solution)/shard_map/all_gather | solution.py:149
  63.9 346.2 %all-gather.12.cloned.1.call-start = ((), (), s32[]{:S(2)}) async-start(), calls=%async_computation.9 | async-start | bytes 14417920 | tf_op jit(solution)/shard_map/all_gather | solution.py:72
  64.5 510.7 %all-reduce.10.cloned.1.call-start = ((), (), s32[]{:S(2)}) async-start(), calls=%async_computation.8 | async-start | bytes 12582912 | tf_op jit(solution)/shard_map/psum | solution.py:181
  64.5 79.5 %collective-permute-start.1 = (bf16[2,512,2816]{2,1,0:T(8,128)(2,1)}, bf16[2,512,2816]{2,1,0:T(8,128)(2,1)}, u32[]{:S(2)}, u32[]{:S(2)}) collective-permute-start(bf16[2,512,2816]{2,1,0:T(8,128)(2,1)} %param.32), channel_id=1, source_target_pairs={{0,8},{8,16},{16,24},{24,0},{1,9},{9,17},{17,25},{25,1},{2,10},{10... | collective-permute-start | bytes 17301512 | tf_op jit(solution)/shard_map/ppermute | solution.py:66
  144.0 137.3 %collective-permute-start.2 = (bf16[2,512,2816]{2,1,0:T(8,128)(2,1)}, bf16[2,512,2816]{2,1,0:T(8,128)(2,1)}, u32[]{:S(2)}, u32[]{:S(2)}) collective-permute-start(bf16[2,512,2816]{2,1,0:T(8,128)(2,1)} %collective-permute-done.1), channel_id=1, source_target_pairs={{0,8},{8,16},{16,24},{24,0},{1,9},{9,17},{17,25},{25,1},{2,10},{10... | collective-permute-start | bytes 17301512 | tf_op jit(solution)/shard_map/ppermute | solution.py:66
  144.2 430.9 %copy-start.66 = (s32[128]{0:T(128)}, s32[128]{0:T(128)S(1)}, u32[]{:S(2)}) copy-start(s32[128]{0:T(128)S(1)} %and_select_fusion) | copy-start | bytes 1540
  144.5 430.7 %copy-start.44 = (s32[768]{0:T(1024)}, s32[768]{0:T(1024)S(1)}, u32[]{:S(2)}) copy-start(s32[768]{0:T(1024)S(1)} %select_reduce_fusion) | copy-start | bytes 9220
  281.3 93.6 %collective-permute-start.3 = (bf16[2,512,2816]{2,1,0:T(8,128)(2,1)}, bf16[2,512,2816]{2,1,0:T(8,128)(2,1)}, u32[]{:S(2)}, u32[]{:S(2)}) collective-permute-start(bf16[2,512,2816]{2,1,0:T(8,128)(2,1)} %collective-permute-done.2), channel_id=1, source_target_pairs={{0,8},{8,16},{16,24},{24,0},{1,9},{9,17},{17,25},{25,1},{2,10},{10... | collective-permute-start | bytes 17301512 | tf_op jit(solution)/shard_map/ppermute | solution.py:66
  301.0 5.6 collective-permute-start
  305.4 274.5 %copy-start.50 = (f32[2048]{0:T(1024)}, f32[2048]{0:T(1024)S(1)}, u32[]{:S(2)}) copy-start(f32[2048]{0:T(1024)S(1)} %convert_element_type.143) | copy-start | bytes 24580
  319.3 517.4 %all-reduce.16.cloned.1.call-start = ((), (), s32[]{:S(2)}) async-start(), calls=%async_computation.14 | async-start | bytes 14155776 | tf_op jit(solution)/shard_map/psum | solution.py:243
  666.1 299.8 %reduce-scatter.2.cloned.1.call-start = ((), (), s32[]{:S(2)}) async-start(), calls=%async_computation.10 | async-start | bytes 4718592 | tf_op jit(solution)/shard_map/reduce_scatter | solution.py:203
  666.1 170.7 %copy-start.51 = (f32[2048]{0:T(1024)S(1)}, f32[2048]{0:T(1024)}, u32[]{:S(2)}) copy-start(f32[2048]{0:T(1024)} %copy-done.50) | copy-start | bytes 24580
  666.1 170.6 %copy-start.55 = (f32[768]{0:T(1024)S(1)}, f32[768]{0:T(1024)}, u32[]{:S(2)}) copy-start(f32[768]{0:T(1024)} %copy-done.54) | copy-start | bytes 9220
  680.6 156.2 %copy-start.33 = (bf16[2048,256]{1,0:T(8,128)(2,1)S(1)}, bf16[2048,256]{1,0:T(8,128)(2,1)}, u32[]{:S(2)}) copy-start(bf16[2048,256]{1,0:T(8,128)(2,1)} %param.38) | copy-start | bytes 3145732
  680.6 380.4 %all-reduce.12.cloned.1.call-start = ((), (), s32[]{:S(2)}) async-start(), calls=%async_computation.12 | async-start | bytes 12582912 | tf_op jit(solution)/shard_map/psum | solution.py:281
  865.6 5.5 collective-permute-start.4
  891.4 397.6 %all-reduce.14.cloned.1.call-start = ((), (), s32[]{:S(2)}) async-start(), calls=%async_computation.13 | async-start | bytes 23330816 | tf_op jit(solution)/shard_map/psum | solution.py:303
  1114.1 177.9 %all-to-all-start.3 = ((bf16[4,192,1024]{2,1,0:T(8,128)(2,1)}), bf16[4,192,1024]{2,1,0:T(8,128)(2,1)}, u32[]{:S(2)}, u32[]{:S(2)}) async-start(bf16[4,192,1024]{2,1,0:T(8,128)(2,1)} %get-tuple-element.66), calls=%async_computation.4 | async-start | bytes 3145728 | tf_op jit(solution)/shard_map/all_to_all | solution.py:297
  (80 other events, 2032.0 us)
Sparse Core Ops, SparseCore 0:
  61.9 46.0 all-gather.5
  109.6 114.2 all-gather.7
  225.4 45.7 all-gather.9
  273.2 44.9 all-gather.13
  319.6 90.4 all-gather.11
  412.4 162.7 all-reduce.9
  666.2 170.5 all-reduce.15
  839.0 43.3 reduce-scatter.1
  891.5 169.4 all-reduce.11
  1066.8 222.1 all-reduce.13
